TPU v7x, 32 devices: a whole 2x2x4 slice. The times are simulated.
32 devices in a mesh: dp: 16 (over z, x, core), tensor: 2 (over y).
Axes of the slice: x: 2, y: 2, z: 4, core: 2. Of those that a mesh axis runs over, the one named last changes fastest.
Arguments:
- hidden_in: bfloat16 [16384, 1024], P(('dp', 'tensor')), may hold values from -6 to 6
- positions: int32 [16384], P('dp'), may hold values from 0 to 1023, as said below
- gain_attention: float32 [1024], replicated, may hold values from 0.1 to 1.9
- gain_feedforward: float32 [1024], replicated, may hold values from 0.1 to 1.9
- gain_query: float32 [128], replicated, may hold values from 0.7 to 5
- gain_key: float32 [128], replicated, may hold values from 0.7 to 5
- query_proj: bfloat16 [1024, 2048], P('dp', 'tensor'), may hold values from -0.1875 to 0.1875
- key_proj: bfloat16 [1024, 1024], P('dp', 'tensor'), may hold values from -0.1875 to 0.1875
- value_proj: bfloat16 [1024, 1024], P('dp', 'tensor'), may hold values from -0.1875 to 0.1875
- out_proj: bfloat16 [2048, 1024], P(('tensor', 'dp')), may hold values from -3 to 3
- gate_proj: bfloat16 [1024, 3072], P('dp', 'tensor'), may hold values from -0.1875 to 0.1875
- up_proj: bfloat16 [1024, 3072], P('dp', 'tensor'), may hold values from -0.1875 to 0.1875
- down_proj: bfloat16 [3072, 1024], P(('tensor', 'dp')), may hold values from -0.21875 to 0.21875
- cotangent: bfloat16 [16384, 1024], P(('dp', 'tensor')), may hold values from -6 to 6
Outputs:
- hidden_out: bfloat16 [16384, 1024], P(('dp', 'tensor'))
- grad_hidden: float32 [16384, 1024], P(('dp', 'tensor'))
- attention_gain_grad: float32 [1024], replicated
- feedforward_gain_grad: float32 [1024], replicated
- query_gain_grad: float32 [128], replicated
- key_gain_grad: float32 [128], replicated
- query_grads: float32 [1024, 2048], P('dp', 'tensor')
- key_grads: float32 [1024, 1024], P('dp', 'tensor')
- value_grads: float32 [1024, 1024], P('dp', 'tensor')
- out_grads: float32 [2048, 1024], P(('tensor', 'dp'))
- gate_grads: float32 [1024, 3072], P('dp', 'tensor')
- up_grads: float32 [1024, 3072], P('dp', 'tensor')
- down_grads: float32 [3072, 1024], P(('tensor', 'dp'))
Inputs may be any that keep to these rules, and one draw needn't show every extreme that they name: Within each sequence of 1024 tokens the positions start at 0 and rise by one from token to token, except that they restart at 0 where a document begins; some sequence holds one document.
All inputs are finite; a program needn't handle non-finite values.
Results may differ from a plain program's by a relative error of at most 0.02.
The roundings to bfloat16 on the way count: a program that leaves them out, or rounds other values in their place, can miss the bound.
Values may be sent and summed in bfloat16 or wider, within the bound.
No kernel may reach another device: no remote copies, remote signals or barrier semaphores. Data moves between devices by JAX's collectives and lax.ppermute only.
A program may use at most 256 MiB of HBM per device.

v0:
```python
import math
import jax
import jax.numpy as jnp
from jax import lax
from jax.sharding import PartitionSpec as P

HD = 128
EPS = 1e-06
THETA = 1000000.0
BF = jnp.bfloat16
F32 = jnp.float32


def rotary_tables(positions, width):
    half_width = width // 2
    freq_index = jnp.arange(half_width).astype(F32)
    inverse_freq = jnp.exp(freq_index * (-2.0 * math.log(THETA) / width))
    angles = positions.astype(F32)[:, None] * inverse_freq[None, :]
    return (jnp.cos(angles)[:, None, :], jnp.sin(angles)[:, None, :])


def rotate(values, cosine_table, sine_table):
    half_width = values.shape[-1] // 2
    lower_half = values[..., :half_width]
    upper_half = values[..., half_width:]
    return jnp.concatenate(
        (
            lower_half * cosine_table - upper_half * sine_table,
            upper_half * cosine_table + lower_half * sine_table,
        ),
        -1,
    )


def rms_unit(values):
    inv_scale = lax.rsqrt(jnp.mean(values * values, -1, keepdims=True) + EPS)
    return (values * inv_scale, inv_scale)


def rms_back(grad_out, gain_vec, unit_vals, inv_scale):
    scaled_grad = grad_out * gain_vec
    return inv_scale * (
        scaled_grad - unit_vals * jnp.mean(scaled_grad * unit_vals, -1, keepdims=True)
    )


def matmul(left, right):
    return jnp.dot(left, right, preferred_element_type=F32)


def contract_rows(left, right):
    return lax.dot_general(left, right, (((0,), (0,)), ((), ())), preferred_element_type=F32)


def contract_cols(left, right):
    return lax.dot_general(left, right, (((1,), (1,)), ((), ())), preferred_element_type=F32)


def attend(query_b, key_b, value_b):
    length = query_b.shape[0]
    block_rows = min(length, 512)
    block_count = length // block_rows
    scale_qk = 1.0 / math.sqrt(query_b.shape[-1])
    outputs = []
    log_sums = []
    for block in range(block_count):
        row_start = block * block_rows
        key_end = row_start + block_rows
        query_block = query_b[row_start:key_end]
        scores = (
            jnp.einsum("qgrd,kgd->grqk", query_block, key_b[:key_end], preferred_element_type=F32)
            * scale_qk
        )
        causal = (row_start + jnp.arange(block_rows, dtype=jnp.int32))[:, None] >= jnp.arange(
            key_end, dtype=jnp.int32
        )[None, :]
        scores = jnp.where(causal, scores, -jnp.inf)
        top_score = jnp.max(scores, -1, keepdims=True)
        shifted = jnp.exp(scores - top_score)
        sum_exp = jnp.sum(shifted, -1, keepdims=True)
        probs_b = (shifted / sum_exp).astype(BF)
        outputs.append(
            jnp.einsum("grqk,kgd->qgrd", probs_b, value_b[:key_end], preferred_element_type=F32)
        )
        log_sums.append(top_score + jnp.log(sum_exp))
    return (jnp.concatenate(outputs, 0), log_sums)


def attend_back(query_b, key_b, value_b, grad_b, log_sums):
    length = query_b.shape[0]
    block_rows = min(length, 512)
    block_count = length // block_rows
    scale_qk = 1.0 / math.sqrt(query_b.shape[-1])
    key_acc = jnp.zeros(key_b.shape, F32)
    value_acc = jnp.zeros(key_b.shape, F32)
    grad_queries = []
    for block in range(block_count):
        row_start = block * block_rows
        key_end = row_start + block_rows
        query_block = query_b[row_start:key_end]
        grad_block = grad_b[row_start:key_end]
        keys_seen = key_b[:key_end]
        scores = (
            jnp.einsum("qgrd,kgd->grqk", query_block, keys_seen, preferred_element_type=F32)
            * scale_qk
        )
        causal = (row_start + jnp.arange(block_rows, dtype=jnp.int32))[:, None] >= jnp.arange(
            key_end, dtype=jnp.int32
        )[None, :]
        scores = jnp.where(causal, scores, -jnp.inf)
        probs = jnp.exp(scores - log_sums[block])
        probs_b = probs.astype(BF)
        grad_probs = jnp.einsum(
            "qgrd,kgd->grqk", grad_block, value_b[:key_end], preferred_element_type=F32
        )
        row_dot = jnp.sum(probs * grad_probs, -1, keepdims=True)
        grad_scores_b = (probs * (grad_probs - row_dot)).astype(BF)
        grad_queries.append(
            jnp.einsum("grqk,kgd->qgrd", grad_scores_b, keys_seen, preferred_element_type=F32)
            * scale_qk
        )
        key_acc = key_acc.at[:key_end].add(
            jnp.einsum("grqk,qgrd->kgd", grad_scores_b, query_block, preferred_element_type=F32)
            * scale_qk
        )
        value_acc = value_acc.at[:key_end].add(
            jnp.einsum("grqk,qgrd->kgd", probs_b, grad_block, preferred_element_type=F32)
        )
    return (jnp.concatenate(grad_queries, 0), key_acc, value_acc)


def all_sum(value, sizes):
    for axis, size in sizes:
        if size & size - 1:
            value = lax.psum(value, axis)
            continue
        step = 1
        while step < size:
            value = value + lax.ppermute(value, axis, [(i, i ^ step) for i in range(size)])
            step *= 2
    return value


def make_local(n_dp, n_tensor):
    paired = n_tensor == 2
    swap = [(0, 1), (1, 0)]

    def gather_rows(own):
        if paired:
            return jnp.concatenate((own, lax.ppermute(own, "tensor", swap)), 0)
        return lax.all_gather(own, "tensor", axis=0, tiled=True)

    def to_sequence(rows):
        if not paired:
            return rows
        half = rows.shape[0] // 2
        first = lax.axis_index("tensor") == 0
        return jnp.concatenate(
            (
                jnp.where(first, rows[:half], rows[half:]),
                jnp.where(first, rows[half:], rows[:half]),
            ),
            0,
        )

    def scatter_rows(part, operand):
        if paired:
            half = operand[0].shape[0] // 2
            sent = part(*(o[half:] for o in operand)).astype(BF)
            got = lax.ppermute(sent, "tensor", swap)
            return part(*(o[:half] for o in operand)) + got.astype(F32)
        return lax.psum_scatter(
            part(*operand).astype(BF), "tensor", scatter_dimension=0, tiled=True
        ).astype(F32)

    def local(
        hidden_in,
        positions,
        gain_attention,
        gain_feedforward,
        gain_query,
        gain_key,
        query_proj,
        key_proj,
        value_proj,
        out_proj,
        gate_proj,
        up_proj,
        down_proj,
        cotangent,
    ):
        length = positions.shape[0]
        own = hidden_in.shape[0]
        width = hidden_in.shape[1]
        heads_here = query_proj.shape[1] // HD
        groups_here = key_proj.shape[1] // HD
        width_query = heads_here * HD
        width_key = groups_here * HD
        width_qkv = width_query + 2 * width_key
        units = gate_proj.shape[1]
        shard_rows = query_proj.shape[0]
        shard_attn = jnp.concatenate(
            (query_proj, key_proj, value_proj, out_proj.reshape(shard_rows, -1)), 1
        )
        shard_mlp = jnp.concatenate((gate_proj, up_proj, down_proj.reshape(shard_rows, -1)), 1)
        full_attn = lax.all_gather(shard_attn, "dp", axis=0, tiled=True)
        full_mlp = lax.all_gather(shard_mlp, "dp", axis=0, tiled=True)
        proj_qkv = full_attn[:, :width_qkv]
        full_out = full_attn[:, width_qkv:].reshape(-1, width)
        full_gateup = full_mlp[:, : 2 * units]
        full_down = full_mlp[:, 2 * units :].reshape(-1, width)
        rows_hidden = gather_rows(hidden_in)
        rows_cot = gather_rows(cotangent)
        cosine_table, sine_table = rotary_tables(positions, HD)
        unit_rows, scale_rows = rms_unit(rows_hidden.astype(F32))
        rows_attn = (unit_rows * gain_attention).astype(BF)
        if paired:
            hidden_f, unit_attn, scale_attn = (
                hidden_in.astype(F32),
                unit_rows[:own],
                scale_rows[:own],
            )
        else:
            hidden_f = hidden_in.astype(F32)
            unit_attn, scale_attn = rms_unit(hidden_f)
        projected = to_sequence(matmul(rows_attn, proj_qkv))
        query_raw = projected[:, :width_query].reshape(length, heads_here, HD)
        key_raw = projected[:, width_query : width_query + width_key].reshape(
            length, groups_here, HD
        )
        value_b = (
            projected[:, width_query + width_key :].astype(BF).reshape(length, groups_here, HD)
        )
        query_unit, query_scale = rms_unit(query_raw)
        key_unit, key_scale = rms_unit(key_raw)
        query_b = (
            rotate(query_unit * gain_query, cosine_table, sine_table)
            .astype(BF)
            .reshape(length, groups_here, heads_here // groups_here, HD)
        )
        key_b = rotate(key_unit * gain_key, cosine_table, sine_table).astype(BF)
        heads_out, log_sums = attend(query_b, key_b, value_b)
        heads_b = to_sequence(heads_out.reshape(length, width_query).astype(BF))
        resid = hidden_f + scatter_rows(lambda h: matmul(h, full_out), (heads_b,))
        unit_mlp, scale_mlp = rms_unit(resid)
        rows_mlp = gather_rows((unit_mlp * gain_feedforward).astype(BF))
        gate_val = matmul(rows_mlp, full_gateup[:, :units])
        up_val = matmul(rows_mlp, full_gateup[:, units:])
        sigmoid_gate = jax.nn.sigmoid(gate_val)
        active_b = (gate_val * sigmoid_gate * up_val).astype(BF)
        output_b = (resid + scatter_rows(lambda a: matmul(a, full_down), (active_b,))).astype(BF)
        grad_active = contract_cols(rows_cot, full_down)
        grad_gate_b = (
            grad_active * up_val * sigmoid_gate * (1.0 + gate_val * (1.0 - sigmoid_gate))
        ).astype(BF)
        grad_up_b = (grad_active * gate_val * sigmoid_gate).astype(BF)
        grad_normed_mlp = scatter_rows(
            lambda g, u: contract_cols(g, full_gateup[:, :units])
            + contract_cols(u, full_gateup[:, units:]),
            (grad_gate_b, grad_up_b),
        )
        grad_mlp_w = jnp.concatenate(
            (
                contract_rows(rows_mlp, grad_gate_b).astype(BF),
                contract_rows(rows_mlp, grad_up_b).astype(BF),
                contract_rows(active_b, rows_cot).astype(BF).reshape(width, -1),
            ),
            1,
        )
        sent_mlp = lax.psum_scatter(grad_mlp_w, "dp", scatter_dimension=0, tiled=True)
        term_feedforward = jnp.sum(grad_normed_mlp * unit_mlp, 0)
        grad_resid = cotangent.astype(F32) + rms_back(
            grad_normed_mlp, gain_feedforward, unit_mlp, scale_mlp
        )
        rows_resid = gather_rows(grad_resid.astype(BF))
        grad_heads_b = to_sequence(contract_cols(rows_resid, full_out).astype(BF)).reshape(
            length, groups_here, heads_here // groups_here, HD
        )
        grad_qrot, grad_krot, grad_value = attend_back(
            query_b, key_b, value_b, grad_heads_b, log_sums
        )
        grad_qnormed = rotate(grad_qrot.reshape(length, heads_here, HD), cosine_table, -sine_table)
        grad_knormed = rotate(grad_krot, cosine_table, -sine_table)
        term_query = jnp.sum(grad_qnormed * query_unit, (0, 1))
        term_key = jnp.sum(grad_knormed * key_unit, (0, 1))
        grad_qkv_b = to_sequence(
            jnp.concatenate(
                (
                    rms_back(grad_qnormed, gain_query, query_unit, query_scale).reshape(
                        length, width_query
                    ),
                    rms_back(grad_knormed, gain_key, key_unit, key_scale).reshape(
                        length, width_key
                    ),
                    grad_value.reshape(length, width_key),
                ),
                1,
            ).astype(BF)
        )
        grad_attn_w = jnp.concatenate(
            (
                contract_rows(rows_attn, grad_qkv_b).astype(BF),
                contract_rows(heads_b, rows_resid).astype(BF).reshape(width, -1),
            ),
            1,
        )
        sent_attn = lax.psum_scatter(grad_attn_w, "dp", scatter_dimension=0, tiled=True)
        grad_normed_attn = scatter_rows(lambda g: contract_cols(g, proj_qkv), (grad_qkv_b,))
        term_attention = jnp.sum(grad_normed_attn * unit_attn, 0)
        grad_hidden = grad_resid + rms_back(grad_normed_attn, gain_attention, unit_attn, scale_attn)
        terms = all_sum(
            jnp.concatenate((term_attention, term_feedforward, term_query, term_key)).reshape(
                -1, HD
            ),
            (("tensor", n_tensor), ("dp", n_dp)),
        ).reshape(-1)
        sent_attn = sent_attn.astype(F32)
        sent_mlp = sent_mlp.astype(F32)
        return (
            output_b,
            grad_hidden,
            terms[:width],
            terms[width : 2 * width],
            terms[2 * width : 2 * width + HD],
            terms[2 * width + HD :],
            sent_attn[:, :width_query],
            sent_attn[:, width_query : width_query + width_key],
            sent_attn[:, width_query + width_key : width_qkv],
            sent_attn[:, width_qkv:].reshape(out_proj.shape),
            sent_mlp[:, :units],
            sent_mlp[:, units : 2 * units],
            sent_mlp[:, 2 * units :].reshape(down_proj.shape),
        )

    return local


def solution(mesh):
    rows = P(("dp", "tensor"), None)
    cut = P("dp", "tensor")
    stacked = P(("tensor", "dp"), None)
    return jax.shard_map(
        make_local(mesh.shape["dp"], mesh.shape["tensor"]),
        mesh=mesh,
        in_specs=(
            rows,
            P("dp"),
            P(),
            P(),
            P(),
            P(),
            cut,
            cut,
            cut,
            stacked,
            cut,
            cut,
            stacked,
            rows,
        ),
        out_specs=(rows, rows, P(), P(), P(), P(), cut, cut, cut, stacked, cut, cut, stacked),
        check_vma=False,
    )
```

profile of v0, /device:TPU:0, one launch (start us, length us, event | category | flops | bytes accessed | tf_op | source)
XLA Modules:
  0.0 633.6 jit_solution(4155793221985874017)
XLA Ops:
  20.3 18.2 %collective-permute-done = bf16[512,1024]{1,0:T(8,128)(2,1)S(1)} collective-permute-done((bf16[512,1024]{1,0:T(8,128)(2,1)S(1)}, bf16[512,1024]{1,0:T(8,128)(2,1)S(1)}, u32[]{:S(2)}, u32[]{:S(2)}) %collective-permute-start) | collective-permute-done | bytes 1048608 | tf_op jit(solution)/shard_map/ppermute | solution.py:150
  39.0 36.1 %all-gather.3.cloned.1.call-done = bf16[1024,3072]{1,0:T(8,128)(2,1)} async-done(((bf16[64,3072]{1,0:T(8,128)(2,1)}), bf16[1024,3072]{1,0:T(8,128)(2,1)}) %all-gather.3.cloned.1.call-update) | async-done | bytes 6291472 | tf_op jit(solution)/shard_map/all_gather | solution.py:206
  75.0 10.0 %fusion.36 = f32[1024,2048]{1,0:T(8,128)} fusion(bf16[1024,3072]{1,0:T(8,128)(2,1)} %all-gather.3.cloned.1.call-done, f32[1024]{0:T(1024)S(1)} %copy-done.74, f32[1024]{0:T(1024)S(1)} %add_rsqrt_fusion.2, bf16[512,1024]{1,0:T(8,128)(2,1)S(1)} %collective-permute-done, bf16[512,1024]{1,0:T(8,128)(2,1)S(1)} %copy-done.40), kind=kOutput, calls=%fused_computation.77 | convolution fusion | flops 4302307328 | bytes 14688256 | tf_op jit(solution)/shard_map/dot_general | solution.py:48
  85.0 4.3 slice_select_fusion.1
  125.7 7.5 %fusion.135 = (f32[4,2,512]{2,1,0:T(2,128)S(1)}, f32[4,2,512,1024]{2,3,1,0:T(8,128)}) fusion(bf16[512,4,2,128]{3,0,2,1:T(8,128)(2,1)S(1)} %bitcast.234, bf16[1024,4,64]{2,0,1:T(8,128)(2,1)S(1)} %get-tuple-element.107, bf16[1024,4,64]{2,0,1:T(8,128)(2,1)S(1)} %get-tuple-element.106, pred[512,1024]{0,1:T(8,128)(4,1)S(1)} %copy-done.58), kind=kOutput, calls=%fused_computation.226 | convolution fusion | flops 1088417792 | bytes 19415040 | tf_op jit(solution)/shard_map/qgrd,kgd->grqk/dot_general | solution.py:71
  133.2 8.3 %fusion.3 = f32[4,2,512]{2,1,0:T(2,128)S(1)} fusion(f32[4,2,512,1024]{2,3,1,0:T(8,128)} %get-tuple-element.129, f32[4,2,512]{2,1,0:T(2,128)S(1)} %get-tuple-element.128), kind=kLoop, calls=%fused_computation.9 | loop fusion | flops 8384512 | bytes 16809984 | tf_op jit(solution)/shard_map/reduce_sum | solution.py:80
  141.6 7.8 %fusion.80 = bf16[4,128,2,512]{3,1,2,0:T(8,128)(2,1)S(1)} fusion(f32[4,2,512,1024]{2,3,1,0:T(8,128)} %get-tuple-element.129, f32[4,2,512]{2,1,0:T(2,128)S(1)} %fusion.3, f32[4,2,512]{2,1,0:T(2,128)S(1)} %get-tuple-element.128, bf16[1024,4,128,1]{2,1,0,3:T(4,128)(2,1)S(1)} %bitcast.237), kind=kOutput, calls=%fused_computation.156 | convolution fusion | flops 1086849024 | bytes 18907136 | tf_op jit(solution)/shard_map/grqk,kgd->qgrd/dot_general | solution.py:83
  157.6 24.0 %collective-permute-done.1 = bf16[512,1024]{1,0:T(8,128)(2,1)S(1)} collective-permute-done((bf16[512,1024]{1,0:T(8,128)(2,1)S(1)}, bf16[512,1024]{1,0:T(8,128)(2,1)S(1)}, u32[]{:S(2)}, u32[]{:S(2)}) %collective-permute-start.1) | collective-permute-done | bytes 1048608 | tf_op jit(solution)/shard_map/ppermute | solution.py:170
  188.9 15.2 %collective-permute-done.4 = bf16[512,1024]{1,0:T(8,128)(2,1)S(1)} collective-permute-done((bf16[512,1024]{1,0:T(8,128)(2,1)S(1)}, bf16[512,1024]{1,0:T(8,128)(2,1)S(1)}, u32[]{:S(2)}, u32[]{:S(2)}) %collective-permute-start.4) | collective-permute-done | bytes 1048608 | tf_op jit(solution)/shard_map/ppermute | solution.py:150
  208.8 5.9 reshape.389
  214.7 8.8 %fusion.136 = f32[1024,1536]{1,0:T(8,128)} fusion(bf16[1024,1024]{1,0:T(8,128)(2,1)} %constant_dynamic-update-slice_fusion, bf16[1536,1024]{1,0:T(8,128)(2,1)} %reshape.389), kind=kOutput, calls=%fused_computation.227 | convolution fusion | flops 3221225472 | bytes 11534336 | tf_op jit(solution)/shard_map/dot_general | solution.py:56
  225.9 8.6 %fusion.42 = f32[1024,1536]{1,0:T(8,128)} fusion(bf16[1024,4608]{1,0:T(8,128)(2,1)} %all-gather.5.cloned.1.call-done, bf16[512,1024]{1,0:T(8,128)(2,1)} %collective-permute-done.2, bf16[512,1024]{1,0:T(8,128)(2,1)} %multiply_convert_fusion.4), kind=kOutput, calls=%fused_computation.83 | convolution fusion | flops 3225419776 | bytes 11534336 | tf_op jit(solution)/shard_map/dot_general | solution.py:48
  234.5 10.6 %multiply_convert_fusion.1 = (bf16[1024,1536]{1,0:T(8,128)(2,1)S(1)}, bf16[1024,1536]{1,0:T(8,128)(2,1)}, bf16[1024,1536]{1,0:T(8,128)(2,1)S(1)}) fusion(f32[1024,1536]{1,0:T(8,128)} %fusion.136, f32[1024,1536]{1,0:T(8,128)} %fusion.42, bf16[1024,4608]{1,0:T(8,128)(2,1)S(1)} %bitcast.242, bf16[512,1024]{1,0:T(8,128)(2,1)} %collective-permute-done.2, ...), kind=kOutput, calls=%fused_computation.34 | convolution fusion | flops 3250585600 | bytes 27262976 | tf_op jit(solution)/shard_map/dot_general | solution.py:48
  252.2 21.1 %collective-permute-done.5 = bf16[512,1024]{1,0:T(8,128)(2,1)S(1)} collective-permute-done((bf16[512,1024]{1,0:T(8,128)(2,1)S(1)}, bf16[512,1024]{1,0:T(8,128)(2,1)S(1)}, u32[]{:S(2)}, u32[]{:S(2)}) %collective-permute-start.5) | collective-permute-done | bytes 1048608 | tf_op jit(solution)/shard_map/ppermute | solution.py:170
  281.0 20.6 %collective-permute-done.6 = bf16[512,1024]{1,0:T(8,128)(2,1)S(1)} collective-permute-done((bf16[512,1024]{1,0:T(8,128)(2,1)}, bf16[512,1024]{1,0:T(8,128)(2,1)S(1)}, u32[]{:S(2)}, u32[]{:S(2)}) %collective-permute-start.6) | collective-permute-done | bytes 1048608 | tf_op jit(solution)/shard_map/ppermute | solution.py:150
  301.6 4.7 convolution_convert_fusion.3
  319.2 11.2 %fusion = (f32[4,2,512]{2,1,0:T(2,128)}, f32[4,1024,512,2]{2,1,3,0:T(8,128)}) fusion(f32[4,2,512,1024]{2,3,1,0:T(8,128)S(1)} %bitcast.217, f32[4,2,512]{2,1,0:T(2,128)} %bitcast.246, bf16[512,4,2,128]{0,3,2,1:T(8,128)(2,1)} %bitcast.230, bf16[1024,4,128,1]{2,1,0,3:T(4,128)(2,1)} %bitcast.236), kind=kOutput, calls=%fused_computation.2 | convolution fusion | flops 1086320640 | bytes 35684352 | tf_op jit(solution)/shard_map/qgrd,kgd->grqk/dot_general | solution.py:113
  330.5 8.4 %fusion.2 = bf16[4,2,512,1024]{2,3,1,0:T(8,128)(2,1)S(1)} fusion(f32[4,1024,512,2]{2,1,3,0:T(8,128)} %get-tuple-element.136, f32[4,2,512,1024]{2,3,1,0:T(8,128)S(1)} %bitcast.217, f32[4,2,512]{2,1,0:T(2,128)} %get-tuple-element.135, f32[4,2,512]{2,1,0:T(2,128)} %bitcast.247), kind=kLoop, calls=%fused_computation.4 | loop fusion | flops 16777216 | bytes 41975808 | tf_op jit(solution)/shard_map/convert_element_type | solution.py:117
  356.0 17.1 %multiply_reduce_fusion = (f32[1024,8]{1,0:T(8,128)S(1)}, f32[1024,8,128]{2,1,0:T(8,128)}) fusion(f32[1024,8,128]{2,1,0:T(8,128)S(1)} %bitcast.221, f32[128]{0:T(128)S(1)} %copy-done.71, f32[1024,8]{1,0:T(8,128)S(1)} %copy-done.27, f32[1024,8,64]{2,1,0:T(8,128)S(1)} %get-tuple-element.89, f32[1024,8,64]{2,1,0:T(8,128)S(1)} %get-tuple-element.88), kind=kLoop, calls=%fused_computation.57 | loop fusion | flops 5234688 | bytes 12648960 | tf_op jit(solution)/shard_map/reduce_sum | solution.py:43
  381.7 9.9 %fusion.59 = bf16[1024,4,128]{0,2,1:T(8,128)(2,1)} fusion(f32[512,4,128]{0,2,1:T(8,128)} %fusion.100, bf16[512,4,2,128]{0,3,2,1:T(8,128)(2,1)S(1)} %bitcast.231, f32[4,2,512,1024]{2,3,1,0:T(8,128)} %get-tuple-element.129, f32[4,2,512]{2,1,0:T(2,128)S(1)} %bitcast.248), kind=kOutput, calls=%fused_computation.112 | convolution fusion | flops 1083179008 | bytes 19939328 | tf_op jit(solution)/shard_map/grqk,qgrd->kgd/dot_general | solution.py:127
  398.5 7.0 %fusion.22 = (f32[1024]{0:T(1024)S(1)}, bf16[1024,1024]{1,0:T(8,128)(2,1)S(1)}) fusion(f32[128,8,8,128]{3,2,1,0:T(8,128)} %bitcast.222, f32[128,8,8,128]{3,2,1,0:T(8,128)S(1)} %bitcast.225, f32[512,2048]{1,0:T(8,128)S(1)} %copy-done.4, f32[512,2048]{1,0:T(8,128)S(1)} %copy-done.2, f32[128,8,8,128]{3,2,1,0:T(8,128)S(1)} %bitcast.224, ...), kind=kLoop, calls=%fused_computation.48 | loop fusion | flops 11533312 | bytes 23076864 | tf_op jit(solution)/shard_map/reduce_sum | solution.py:284
  411.7 4.5 fusion.60
  416.3 5.3 fusion.29
  426.6 6.7 %convolution_convert_fusion = bf16[1536,1024]{1,0:T(8,128)(2,1)} fusion(bf16[1024,1536]{1,0:T(8,128)(2,1)S(1)} %copy-done.84, bf16[1024,1024]{1,0:T(8,128)(2,1)} %constant_dynamic-update-slice_fusion), kind=kOutput, calls=%fused_computation.70 | convolution fusion | flops 3222798336 | bytes 8388608 | tf_op jit(solution)/shard_map/dot_general | solution.py:52
  433.3 4.6 reshape.393
  437.9 6.5 %convolution_convert_fusion.2 = bf16[1024,1536]{1,0:T(8,128)(2,1)S(1)} fusion(bf16[1024,1536]{1,0:T(8,128)(2,1)} %copy-done.83, bf16[512,1024]{1,0:T(8,128)(2,1)} %collective-permute-done.2, bf16[512,1024]{1,0:T(8,128)(2,1)} %multiply_convert_fusion.4), kind=kOutput, calls=%fused_computation.72 | convolution fusion | flops 3226992640 | bytes 8388608 | tf_op jit(solution)/shard_map/dot_general | solution.py:52
  444.4 5.4 convolution_convert_fusion.1
  449.9 5.3 pad_maximum_fusion.1
  456.8 4.7 fusion.87
  467.8 19.8 %collective-permute-done.7 = bf16[512,1024]{1,0:T(8,128)(2,1)S(1)} collective-permute-done((bf16[512,1024]{1,0:T(8,128)(2,1)S(1)}, bf16[512,1024]{1,0:T(8,128)(2,1)S(1)}, u32[]{:S(2)}, u32[]{:S(2)}) %collective-permute-start.7) | collective-permute-done | bytes 1048608 | tf_op jit(solution)/shard_map/ppermute | solution.py:170
  491.9 15.5 %collective-permute-done.8 = f32[18,128]{1,0:T(8,128)S(1)} collective-permute-done((f32[18,128]{1,0:T(8,128)S(1)}, f32[18,128]{1,0:T(8,128)S(1)}, u32[]{:S(2)}, u32[]{:S(2)}) %collective-permute-start.8) | collective-permute-done | bytes 9248 | tf_op jit(solution)/shard_map/ppermute | solution.py:139
  526.2 97.4 %reduce-scatter.5.cloned.1.call-done = bf16[64,4608]{1,0:T(8,128)(2,1)} async-done(((bf16[1024,4608]{1,0:T(8,128)(2,1)}), bf16[64,4608]{1,0:T(8,128)(2,1)}) %reduce-scatter.5.cloned.1.call-update) | async-done | bytes 589840 | tf_op jit(solution)/shard_map/reduce_scatter | solution.py:270
  (346 shorter events, 176.9 us)
Async XLA Ops:
  7.2 67.8 %all-gather.3.cloned.1.call-start = ((), (), s32[]{:S(2)}) async-start(), calls=%async_computation.2 | async-start | bytes 6684672 | tf_op jit(solution)/shard_map/all_gather | solution.py:206
  9.2 195.9 %all-gather.5.cloned.1.call-start = ((), (), s32[]{:S(2)}) async-start(), calls=%async_computation.3 | async-start | bytes 10027008 | tf_op jit(solution)/shard_map/all_gather | solution.py:207
  10.3 64.8 %copy-start.74 = (f32[1024]{0:T(1024)S(1)}, f32[1024]{0:T(1024)}, u32[]{:S(2)}) copy-start(f32[1024]{0:T(1024)} %param.28) | copy-start | bytes 12292
  12.2 510.6 %reduce-scatter.3.cloned.1.call-start = ((), (), s32[]{:S(2)}) async-start(), calls=%async_computation.4 | async-start | bytes 6684672 | tf_op jit(solution)/shard_map/reduce_scatter | solution.py:307
  12.2 26.2 %collective-permute-start = (bf16[512,1024]{1,0:T(8,128)(2,1)S(1)}, bf16[512,1024]{1,0:T(8,128)(2,1)S(1)}, u32[]{:S(2)}, u32[]{:S(2)}) collective-permute-start(bf16[512,1024]{1,0:T(8,128)(2,1)S(1)} %copy-done.40), channel_id=1, source_target_pairs={{0,1},{1,0},{2,3},{3,2},{4,5},{5,4},{6,7},{7,6},{8,9},{9,8},{10,11... | collective-permute-start | bytes 3145736 | tf_op jit(solution)/shard_map/ppermute | solution.py:150
  20.3 79.7 %copy-start.15 = (f32[1024,64]{1,0:T(8,128)}, f32[1024,64]{1,0:T(8,128)S(1)}, u32[]{:S(2)}) copy-start(f32[1024,64]{1,0:T(8,128)S(1)} %get-tuple-element.125) | copy-start | bytes 786436
  20.3 79.7 %copy-start.34 = (f32[1024,64]{1,0:T(8,128)}, f32[1024,64]{1,0:T(8,128)S(1)}, u32[]{:S(2)}) copy-start(f32[1024,64]{1,0:T(8,128)S(1)} %get-tuple-element.124) | copy-start | bytes 786436
  38.5 46.6 %copy-start.44 = (bf16[512,1024]{1,0:T(8,128)(2,1)}, bf16[512,1024]{1,0:T(8,128)(2,1)S(1)}, u32[]{:S(2)}) copy-start(bf16[512,1024]{1,0:T(8,128)(2,1)S(1)} %collective-permute-done) | copy-start | bytes 3145732
  39.0 46.1 %copy-start.67 = (f32[1024]{0:T(1024)}, f32[1024]{0:T(1024)S(1)}, u32[]{:S(2)}) copy-start(f32[1024]{0:T(1024)S(1)} %add_rsqrt_fusion.2) | copy-start | bytes 12292
  117.9 161.4 %copy-start.60 = (f32[1024,4]{0,1:T(4,128)}, f32[1024,4]{0,1:T(4,128)S(1)}, u32[]{:S(2)}) copy-start(f32[1024,4]{0,1:T(4,128)S(1)} %add_rsqrt_fusion.1) | copy-start | bytes 49156
  151.8 29.8 %copy-start.79 = (bf16[4,128,2,512]{3,1,2,0:T(8,128)(2,1)}, bf16[4,128,2,512]{3,1,2,0:T(8,128)(2,1)S(1)}, u32[]{:S(2)}) copy-start(bf16[4,128,2,512]{3,1,2,0:T(8,128)(2,1)S(1)} %get-tuple-element.110) | copy-start | bytes 3145732
  151.8 29.8 %copy-start.41 = (bf16[512,1024]{1,0:T(8,128)(2,1)S(1)}, bf16[512,1024]{1,0:T(8,128)(2,1)}, u32[]{:S(2)}) copy-start(bf16[512,1024]{1,0:T(8,128)(2,1)} %param.26) | copy-start | bytes 3145732
  155.5 26.1 %collective-permute-start.1 = (bf16[512,1024]{1,0:T(8,128)(2,1)S(1)}, bf16[512,1024]{1,0:T(8,128)(2,1)S(1)}, u32[]{:S(2)}, u32[]{:S(2)}) collective-permute-start(bf16[512,1024]{1,0:T(8,128)(2,1)S(1)} %fusion.84), channel_id=1, source_target_pairs={{0,1},{1,0},{2,3},{3,2},{4,5},{5,4},{6,7},{7,6},{8,9},{9,8},{10,11... | collective-permute-start | bytes 3145736 | tf_op jit(solution)/shard_map/ppermute | solution.py:170
  157.1 46.9 %collective-permute-start.4 = (bf16[512,1024]{1,0:T(8,128)(2,1)S(1)}, bf16[512,1024]{1,0:T(8,128)(2,1)S(1)}, u32[]{:S(2)}, u32[]{:S(2)}) collective-permute-start(bf16[512,1024]{1,0:T(8,128)(2,1)S(1)} %copy-done.23), channel_id=1, source_target_pairs={{0,1},{1,0},{2,3},{3,2},{4,5},{5,4},{6,7},{7,6},{8,9},{9,8},{10,11... | collective-permute-start | bytes 3145736 | tf_op jit(solution)/shard_map/ppermute | solution.py:150
  184.7 91.4 %copy-start.10 = (f32[512,1024]{1,0:T(8,128)}, f32[512,1024]{1,0:T(8,128)S(1)}, u32[]{:S(2)}) copy-start(f32[512,1024]{1,0:T(8,128)S(1)} %get-tuple-element.131) | copy-start | bytes 6291460
  184.7 91.4 %copy-start.65 = (f32[512]{0:T(512)}, f32[512]{0:T(512)S(1)}, u32[]{:S(2)}) copy-start(f32[512]{0:T(512)S(1)} %add_rsqrt_fusion.3) | copy-start | bytes 6148
  186.3 39.6 %collective-permute-start.2 = (bf16[512,1024]{1,0:T(8,128)(2,1)}, bf16[512,1024]{1,0:T(8,128)(2,1)}, u32[]{:S(2)}, u32[]{:S(2)}) collective-permute-start(bf16[512,1024]{1,0:T(8,128)(2,1)} %multiply_convert_fusion.4), channel_id=1, source_target_pairs={{0,1},{1,0},{2,3},{3,2},{4,5},{5,4},{6,7},{7,6},{8,9},{9,8},{10,11... | collective-permute-start | bytes 3145736 | tf_op jit(solution)/shard_map/ppermute | solution.py:150
  245.1 28.2 %copy-start.83 = (bf16[1024,1536]{1,0:T(8,128)(2,1)}, bf16[1024,1536]{1,0:T(8,128)(2,1)S(1)}, u32[]{:S(2)}) copy-start(bf16[1024,1536]{1,0:T(8,128)(2,1)S(1)} %get-tuple-element.85) | copy-start | bytes 9437188
  248.8 24.5 %collective-permute-start.5 = (bf16[512,1024]{1,0:T(8,128)(2,1)S(1)}, bf16[512,1024]{1,0:T(8,128)(2,1)S(1)}, u32[]{:S(2)}, u32[]{:S(2)}) collective-permute-start(bf16[512,1024]{1,0:T(8,128)(2,1)S(1)} %add_convert_fusion.1), channel_id=1, source_target_pairs={{0,1},{1,0},{2,3},{3,2},{4,5},{5,4},{6,7},{7,6},{8,9},{9,8},{10,11... | collective-permute-start | bytes 3145736 | tf_op jit(solution)/shard_map/ppermute | solution.py:170
  277.8 23.8 %collective-permute-start.6 = (bf16[512,1024]{1,0:T(8,128)(2,1)}, bf16[512,1024]{1,0:T(8,128)(2,1)S(1)}, u32[]{:S(2)}, u32[]{:S(2)}) collective-permute-start(bf16[512,1024]{1,0:T(8,128)(2,1)} %fusion.128), channel_id=1, source_target_pairs={{0,1},{1,0},{2,3},{3,2},{4,5},{5,4},{6,7},{7,6},{8,9},{9,8},{10,11... | collective-permute-start | bytes 3145736 | tf_op jit(solution)/shard_map/ppermute | solution.py:150
  280.3 27.1 %slice-start.2 = ((s8[8388608]{0:T(1024)(128)(4,1)}), s8[4194304]{0:T(1024)(128)(4,1)S(1)}, s32[]{:S(2)}) async-start(s8[8388608]{0:T(1024)(128)(4,1)} %bitcast.214), calls=%async_computation.8 | async-start | bytes 8388608
  281.0 26.5 %slice-start.3 = ((s8[8388608]{0:T(1024)(128)(4,1)}), s8[4194304]{0:T(1024)(128)(4,1)S(1)}, s32[]{:S(2)}) async-start(s8[8388608]{0:T(1024)(128)(4,1)} %bitcast.214), calls=%async_computation.9 | async-start | bytes 8388608
  424.7 198.9 %reduce-scatter.5.cloned.1.call-start = ((), (), s32[]{:S(2)}) async-start(), calls=%async_computation.5 | async-start | bytes 10027008 | tf_op jit(solution)/shard_map/reduce_scatter | solution.py:270
  461.5 26.1 %collective-permute-start.7 = (bf16[512,1024]{1,0:T(8,128)(2,1)S(1)}, bf16[512,1024]{1,0:T(8,128)(2,1)S(1)}, u32[]{:S(2)}, u32[]{:S(2)}) collective-permute-start(bf16[512,1024]{1,0:T(8,128)(2,1)S(1)} %fusion.87), channel_id=1, source_target_pairs={{0,1},{1,0},{2,3},{3,2},{4,5},{5,4},{6,7},{7,6},{8,9},{9,8},{10,11... | collective-permute-start | bytes 3145736 | tf_op jit(solution)/shard_map/ppermute | solution.py:170
  463.0 24.5 %slice-start.15 = ((s8[6291456]{0:T(1024)(128)(4,1)}), s8[4194304]{0:T(1024)(128)(4,1)S(1)}, s32[]{:S(2)}) async-start(s8[6291456]{0:T(1024)(128)(4,1)} %bitcast.253), calls=%async_computation.21 | async-start | bytes 8388608
  466.1 44.4 %collective-permute-start.3 = (bf16[512,1024]{1,0:T(8,128)(2,1)S(1)}, bf16[512,1024]{1,0:T(8,128)(2,1)S(1)}, u32[]{:S(2)}, u32[]{:S(2)}) collective-permute-start(bf16[512,1024]{1,0:T(8,128)(2,1)S(1)} %fusion.81), channel_id=1, source_target_pairs={{0,1},{1,0},{2,3},{3,2},{4,5},{5,4},{6,7},{7,6},{8,9},{9,8},{10,11... | collective-permute-start | bytes 3145736 | tf_op jit(solution)/shard_map/ppermute | solution.py:170
  467.7 42.8 %copy-start.11 = (f32[512,1024]{1,0:T(8,128)S(1)}, f32[512,1024]{1,0:T(8,128)}, u32[]{:S(2)}) copy-start(f32[512,1024]{1,0:T(8,128)} %copy-done.10) | copy-start | bytes 6291460
  490.3 17.1 %collective-permute-start.8 = (f32[18,128]{1,0:T(8,128)S(1)}, f32[18,128]{1,0:T(8,128)S(1)}, u32[]{:S(2)}, u32[]{:S(2)}) collective-permute-start(f32[18,128]{1,0:T(8,128)S(1)} %maximum_bitcast_fusion.3), channel_id=1, source_target_pairs={{0,1},{1,0},{2,3},{3,2},{4,5},{5,4},{6,7},{7,6},{8,9},{9,8},{10,11... | collective-permute-start | bytes 27656 | tf_op jit(solution)/shard_map/ppermute | solution.py:139
  507.5 1.2 collective-permute-start.9
  508.7 4.6 collective-permute-start.10
  513.3 3.7 collective-permute-start.11
  517.0 4.6 collective-permute-start.12
  (91 other events, 617.2 us)
Sparse Core Ops, SparseCore 0:
  10.9 64.1 all-gather.2
  77.3 79.5 all-gather.4
  424.8 84.4 reduce-scatter.2
  513.3 110.3 reduce-scatter.4
where the time goes:
time: 643 us; the launch traced here: 634 us
  waiting for transfers between devices  274 us (43%)
  matrix products  152 us (24%)
  other arithmetic  101 us (16%)
  local copies, waits for them, and re-layouts  70.6 us (11%)
  starting transfers between devices  19.5 us (3%)
  between operations  15.5 us (2%)
    reduce_scatter x1, waiting for transfers between devices, local(): lax.psum_scatter(grad_mlp_w, 'dp', scatter_dimension=0, tiled=True)  97.4 us
    ppermute x4, waiting for transfers between devices, scatter_rows(): got = lax.ppermute(sent, 'tensor', swap)  64.9 us
    ppermute x4, waiting for transfers between devices, gather_rows(): return jnp.concatenate((own, lax.ppermute(own, 'tensor', swap)), 0)  56.4 us
    dot_general x7, matrix products, matmul(): return jnp.dot(left, right, preferred_element_type=F32)  40.6 us
    all_gather x1, waiting for transfers between devices, local(): full_attn = lax.all_gather(shard_attn, 'dp', axis=0, tiled=True)  36.1 us
    dot_general x8, matrix products, contract_cols(): lax.dot_general(left, right, (((1,), (1,)), ((), ())), preferred_element_...  29.2 us
    dot_general x5, matrix products, contract_rows(): lax.dot_general(left, right, (((0,), (0,)), ((), ())), preferred_element_...  28.4 us
    unnamed x213, local copies, waits for them, and re-layouts  23.4 us
  transfers between devices with their start and end apart: 17, of which 13 were waited for; matrix products, arithmetic and copies ran while one was open for 26% of the time, Pallas kernels for 0%

commit v1 on v0

--- a/solution.py
+++ b/solution.py
@@ -203,7 +203,22 @@
             (query_proj, key_proj, value_proj, out_proj.reshape(shard_rows, -1)), 1
         )
         shard_mlp = jnp.concatenate((gate_proj, up_proj, down_proj.reshape(shard_rows, -1)), 1)
-        full_attn = lax.all_gather(shard_attn, "dp", axis=0, tiled=True)
+        parts_out, m_next, high = (lax.psum(1, "dp"), lax.axis_index("dp"), shard_attn.shape[0])
+        far_arr, answer = (shard_attn, 1)
+        while answer < parts_out:
+            far_arr = jnp.concatenate(
+                [
+                    far_arr,
+                    lax.ppermute(
+                        far_arr,
+                        "dp",
+                        tuple(((k0, (k0 - answer) % parts_out) for k0 in range(parts_out))),
+                    ),
+                ],
+                0,
+            )
+            answer = 2 * answer
+        full_attn = jnp.roll(far_arr, m_next * high, 0)
         full_mlp = lax.all_gather(shard_mlp, "dp", axis=0, tiled=True)
         proj_qkv = full_attn[:, :width_qkv]
         full_out = full_attn[:, width_qkv:].reshape(-1, width)

time: 643 us -> 858 us (1.33)
  waiting for transfers between devices: 274 us -> 457 us
  local copies, waits for them, and re-layouts: 70.6 us -> 89.7 us
    ppermute x0 -> x4, waiting for transfers between devices: none -> 225 us  [local(): lax.ppermute(far_arr, 'dp', tuple(((k0, (k0 - answer) % parts_out) for k0...]
    all_gather x1 -> x0, waiting for transfers between devices: 36.1 us -> none  [local(): full_attn = lax.all_gather(shard_attn, 'dp', axis=0, tiled=True)]
    unnamed x213 -> x217, local copies, waits for them, and re-layouts: 23.4 us -> 37.4 us
  transfers between devices with their start and end apart: 17 -> 20, of which waited for: 13 -> 16; matrix products, arithmetic and copies ran while one was open for 26% -> 22% of each run, Pallas kernels for 0% -> 0%
where the time goes in v1:
time: 858 us; the launch traced here: 847 us
  waiting for transfers between devices  457 us (53%)
  matrix products  157 us (18%)
  other arithmetic  105 us (12%)
  local copies, waits for them, and re-layouts  89.7 us (10%)
  starting transfers between devices  23.4 us (3%)
  between operations  15.4 us (2%)
    ppermute x4, waiting for transfers between devices, local(): lax.ppermute(far_arr, 'dp', tuple(((k0, (k0 - answer) % parts_out) for k0...  225 us
    reduce_scatter x1, waiting for transfers between devices, local(): lax.psum_scatter(grad_mlp_w, 'dp', scatter_dimension=0, tiled=True)  97.8 us
    ppermute x4, waiting for transfers between devices, scatter_rows(): got = lax.ppermute(sent, 'tensor', swap)  63.9 us
    ppermute x4, waiting for transfers between devices, gather_rows(): return jnp.concatenate((own, lax.ppermute(own, 'tensor', swap)), 0)  51.7 us
    dot_general x7, matrix products, matmul(): return jnp.dot(left, right, preferred_element_type=F32)  41.5 us
    unnamed x217, local copies, waits for them, and re-layouts  37.4 us
    dot_general x8, matrix products, contract_cols(): lax.dot_general(left, right, (((1,), (1,)), ((), ())), preferred_element_...  31.3 us
    dot_general x5, matrix products, contract_rows(): lax.dot_general(left, right, (((0,), (0,)), ((), ())), preferred_element_...  30.1 us
  transfers between devices with their start and end apart: 20, of which 16 were waited for; matrix products, arithmetic and copies ran while one was open for 22% of the time, Pallas kernels for 0%

profile of v1, /device:TPU:0, one launch (start us, length us, event | category | flops | bytes accessed | tf_op | source)
XLA Modules:
  0.0 847.2 jit_solution(1728065280918379921)
XLA Ops:
  13.4 5.4 collective-permute-start.1
  18.8 5.3 collective-permute-done.1
  24.8 17.3 %collective-permute-done.2 = bf16[128,3072]{1,0:T(8,128)(2,1)S(1)} collective-permute-done((bf16[128,3072]{1,0:T(8,128)(2,1)S(1)}, bf16[128,3072]{1,0:T(8,128)(2,1)S(1)}, u32[]{:S(2)}, u32[]{:S(2)}) %collective-permute-start.2) | collective-permute-done | bytes 786464 | tf_op jit(solution)/shard_map/ppermute | solution.py:212
  42.8 36.5 %collective-permute-done.3 = bf16[256,3072]{1,0:T(8,128)(2,1)S(1)} collective-permute-done((bf16[256,3072]{1,0:T(8,128)(2,1)S(1)}, bf16[256,3072]{1,0:T(8,128)(2,1)S(1)}, u32[]{:S(2)}, u32[]{:S(2)}) %collective-permute-start.3) | collective-permute-done | bytes 1572896 | tf_op jit(solution)/shard_map/ppermute | solution.py:212
  92.6 14.3 %collective-permute-done = bf16[512,1024]{1,0:T(8,128)(2,1)} collective-permute-done((bf16[512,1024]{1,0:T(8,128)(2,1)}, bf16[512,1024]{1,0:T(8,128)(2,1)}, u32[]{:S(2)}, u32[]{:S(2)}) %collective-permute-start) | collective-permute-done | bytes 1048608 | tf_op jit(solution)/shard_map/ppermute | solution.py:150
  111.1 165.5 %collective-permute-done.4 = bf16[512,3072]{1,0:T(8,128)(2,1)} collective-permute-done((bf16[512,3072]{1,0:T(8,128)(2,1)}, bf16[512,3072]{1,0:T(8,128)(2,1)}, u32[]{:S(2)}, u32[]{:S(2)}) %collective-permute-start.4) | collective-permute-done | bytes 3145760 | tf_op jit(solution)/shard_map/ppermute | solution.py:212
  289.9 10.7 %fusion.36 = f32[1024,2048]{1,0:T(8,128)} fusion(bf16[2048,3072]{1,0:T(8,128)(2,1)} %constant_dynamic-update-slice_fusion.4, s32[]{:T(128)S(6)} %select_n.76, f32[1024]{0:T(1024)S(1)} %copy-done.71, f32[1024]{0:T(1024)S(1)} %add_rsqrt_fusion.2, bf16[512,1024]{1,0:T(8,128)(2,1)} %collective-permute-done, bf16[512,1024]{1,0:T(8,128)(2,1)} %param.26), kind=kOutput, calls=%fused_computation.77 | convolution fusion | flops 4302307328 | bytes 14688260 | tf_op jit(solution)/shard_map/dot_general | solution.py:48
  340.5 7.5 fusion.140
  348.0 8.2 fusion.3
  356.2 7.8 fusion.82
  371.9 24.0 %collective-permute-done.5 = bf16[512,1024]{1,0:T(8,128)(2,1)S(1)} collective-permute-done((bf16[512,1024]{1,0:T(8,128)(2,1)S(1)}, bf16[512,1024]{1,0:T(8,128)(2,1)S(1)}, u32[]{:S(2)}, u32[]{:S(2)}) %collective-permute-start.5) | collective-permute-done | bytes 1048608 | tf_op jit(solution)/shard_map/ppermute | solution.py:170
  403.4 15.0 %collective-permute-done.8 = bf16[512,1024]{1,0:T(8,128)(2,1)S(1)} collective-permute-done((bf16[512,1024]{1,0:T(8,128)(2,1)S(1)}, bf16[512,1024]{1,0:T(8,128)(2,1)S(1)}, u32[]{:S(2)}, u32[]{:S(2)}) %collective-permute-start.8) | collective-permute-done | bytes 1048608 | tf_op jit(solution)/shard_map/ppermute | solution.py:150
  423.3 5.9 reshape.389
  429.2 8.7 %fusion.141 = f32[1024,1536]{1,0:T(8,128)} fusion(bf16[1024,1024]{1,0:T(8,128)(2,1)} %constant_dynamic-update-slice_fusion.17, bf16[1536,1024]{1,0:T(8,128)(2,1)} %reshape.389), kind=kOutput, calls=%fused_computation.252 | convolution fusion | flops 3221225472 | bytes 11534336 | tf_op jit(solution)/shard_map/dot_general | solution.py:56
  440.0 8.5 %fusion.42 = f32[1024,1536]{1,0:T(8,128)} fusion(bf16[1024,4608]{1,0:T(8,128)(2,1)} %all-gather.2.cloned.1.call-done, bf16[512,1024]{1,0:T(8,128)(2,1)} %collective-permute-done.6, bf16[512,1024]{1,0:T(8,128)(2,1)} %multiply_convert_fusion.4), kind=kOutput, calls=%fused_computation.84 | convolution fusion | flops 3225419776 | bytes 11534336 | tf_op jit(solution)/shard_map/dot_general | solution.py:48
  448.6 10.6 %multiply_convert_fusion.1 = (bf16[1024,1536]{1,0:T(8,128)(2,1)S(1)}, bf16[1024,1536]{1,0:T(8,128)(2,1)}, bf16[1024,1536]{1,0:T(8,128)(2,1)S(1)}) fusion(f32[1024,1536]{1,0:T(8,128)} %fusion.141, f32[1024,1536]{1,0:T(8,128)} %fusion.42, bf16[1024,4608]{1,0:T(8,128)(2,1)S(1)} %bitcast.242, bf16[512,1024]{1,0:T(8,128)(2,1)} %collective-permute-done.6, ...), kind=kOutput, calls=%fused_computation.34 | convolution fusion | flops 3250585600 | bytes 27262976 | tf_op jit(solution)/shard_map/dot_general | solution.py:48
  466.3 20.8 %collective-permute-done.9 = bf16[512,1024]{1,0:T(8,128)(2,1)S(1)} collective-permute-done((bf16[512,1024]{1,0:T(8,128)(2,1)S(1)}, bf16[512,1024]{1,0:T(8,128)(2,1)S(1)}, u32[]{:S(2)}, u32[]{:S(2)}) %collective-permute-start.9) | collective-permute-done | bytes 1048608 | tf_op jit(solution)/shard_map/ppermute | solution.py:170
  494.9 20.3 %collective-permute-done.10 = bf16[512,1024]{1,0:T(8,128)(2,1)S(1)} collective-permute-done((bf16[512,1024]{1,0:T(8,128)(2,1)}, bf16[512,1024]{1,0:T(8,128)(2,1)S(1)}, u32[]{:S(2)}, u32[]{:S(2)}) %collective-permute-start.10) | collective-permute-done | bytes 1048608 | tf_op jit(solution)/shard_map/ppermute | solution.py:150
  533.0 11.2 %fusion = (f32[4,2,512]{2,1,0:T(2,128)}, f32[4,1024,512,2]{2,1,3,0:T(8,128)}) fusion(f32[4,2,512,1024]{2,3,1,0:T(8,128)S(1)} %bitcast.217, f32[4,2,512]{2,1,0:T(2,128)} %bitcast.246, bf16[512,4,2,128]{0,3,2,1:T(8,128)(2,1)} %bitcast.230, bf16[1024,4,128,1]{2,1,0,3:T(4,128)(2,1)} %bitcast.236), kind=kOutput, calls=%fused_computation.2 | convolution fusion | flops 1086320640 | bytes 35684352 | tf_op jit(solution)/shard_map/qgrd,kgd->grqk/dot_general | solution.py:113
  544.3 8.4 fusion.2
  569.7 16.9 %multiply_reduce_fusion = (f32[1024,8]{1,0:T(8,128)S(1)}, f32[1024,8,128]{2,1,0:T(8,128)}) fusion(f32[1024,8,128]{2,1,0:T(8,128)S(1)} %bitcast.221, f32[128]{0:T(128)S(1)} %copy-done.68, f32[1024,8]{1,0:T(8,128)S(1)} %copy-done.26, f32[1024,8,64]{2,1,0:T(8,128)S(1)} %get-tuple-element.89, f32[1024,8,64]{2,1,0:T(8,128)S(1)} %get-tuple-element.88), kind=kLoop, calls=%fused_computation.57 | loop fusion | flops 5234688 | bytes 12648960 | tf_op jit(solution)/shard_map/reduce_sum | solution.py:43
  595.3 10.0 %fusion.59 = bf16[1024,4,128]{0,2,1:T(8,128)(2,1)} fusion(f32[512,4,128]{0,2,1:T(8,128)} %fusion.102, bf16[512,4,2,128]{0,3,2,1:T(8,128)(2,1)S(1)} %bitcast.231, f32[4,2,512,1024]{2,3,1,0:T(8,128)} %get-tuple-element.137, f32[4,2,512]{2,1,0:T(2,128)S(1)} %bitcast.248), kind=kOutput, calls=%fused_computation.113 | convolution fusion | flops 1083179008 | bytes 19939328 | tf_op jit(solution)/shard_map/grqk,qgrd->kgd/dot_general | solution.py:127
  611.3 7.1 fusion.22
  629.0 6.8 fusion.29
  640.8 6.9 convolution_convert_fusion
  652.4 6.5 convolution_convert_fusion.2
  658.9 5.4 convolution_convert_fusion.1
  664.3 5.2 pad_maximum_fusion.1
  682.7 19.1 %collective-permute-done.11 = bf16[512,1024]{1,0:T(8,128)(2,1)S(1)} collective-permute-done((bf16[512,1024]{1,0:T(8,128)(2,1)S(1)}, bf16[512,1024]{1,0:T(8,128)(2,1)S(1)}, u32[]{:S(2)}, u32[]{:S(2)}) %collective-permute-start.11) | collective-permute-done | bytes 1048608 | tf_op jit(solution)/shard_map/ppermute | solution.py:170
  701.8 5.1 multiply_reduce_fusion.3
  708.6 12.7 %collective-permute-done.12 = f32[18,128]{1,0:T(8,128)S(1)} collective-permute-done((f32[18,128]{1,0:T(8,128)S(1)}, f32[18,128]{1,0:T(8,128)S(1)}, u32[]{:S(2)}, u32[]{:S(2)}) %collective-permute-start.12) | collective-permute-done | bytes 9248 | tf_op jit(solution)/shard_map/ppermute | solution.py:139
  739.7 97.8 %reduce-scatter.5.cloned.1.call-done = bf16[64,4608]{1,0:T(8,128)(2,1)} async-done(((bf16[1024,4608]{1,0:T(8,128)(2,1)}), bf16[64,4608]{1,0:T(8,128)(2,1)}) %reduce-scatter.5.cloned.1.call-update) | async-done | bytes 589840 | tf_op jit(solution)/shard_map/reduce_scatter | solution.py:285
  (357 shorter events, 220.3 us)
Async XLA Ops:
  7.2 412.3 %all-gather.2.cloned.1.call-start = ((), (), s32[]{:S(2)}) async-start(), calls=%async_computation.2 | async-start | bytes 10027008 | tf_op jit(solution)/shard_map/all_gather | solution.py:222
  13.4 10.7 %collective-permute-start.1 = (bf16[64,3072]{1,0:T(8,128)(2,1)S(1)}, bf16[64,3072]{1,0:T(8,128)(2,1)S(1)}, u32[]{:S(2)}, u32[]{:S(2)}) collective-permute-start(bf16[64,3072]{1,0:T(8,128)(2,1)S(1)} %get-tuple-element.119), channel_id=1, source_target_pairs={{0,30},{2,0},{4,2},{6,4},{8,6},{10,8},{12,10},{14,12},{16,14},{18,... | collective-permute-start | bytes 1179656 | tf_op jit(solution)/shard_map/ppermute | solution.py:212
  24.2 60.6 %copy-start.58 = (bf16[64,1536]{1,0:T(8,128)(2,1)S(1)}, bf16[64,1536]{1,0:T(8,128)(2,1)}, u32[]{:S(2)}) copy-start(bf16[64,1536]{1,0:T(8,128)(2,1)} %param.37) | copy-start | bytes 589828
  24.2 17.9 %collective-permute-start.2 = (bf16[128,3072]{1,0:T(8,128)(2,1)S(1)}, bf16[128,3072]{1,0:T(8,128)(2,1)S(1)}, u32[]{:S(2)}, u32[]{:S(2)}) collective-permute-start(bf16[128,3072]{1,0:T(8,128)(2,1)S(1)} %pad_maximum_fusion.15), channel_id=1, source_target_pairs={{0,28},{2,30},{4,0},{6,2},{8,4},{10,6},{12,8},{14,10},{16,12},{18,... | collective-permute-start | bytes 2359304 | tf_op jit(solution)/shard_map/ppermute | solution.py:212
  42.2 44.5 %copy-start.73 = (s32[1024]{0:T(1024)S(1)}, s32[1024]{0:T(1024)}, u32[]{:S(2)}) copy-start(s32[1024]{0:T(1024)} %param.27) | copy-start | bytes 12292
  42.2 37.1 %collective-permute-start.3 = (bf16[256,3072]{1,0:T(8,128)(2,1)S(1)}, bf16[256,3072]{1,0:T(8,128)(2,1)S(1)}, u32[]{:S(2)}, u32[]{:S(2)}) collective-permute-start(bf16[256,3072]{1,0:T(8,128)(2,1)S(1)} %pad_maximum_fusion.11), channel_id=1, source_target_pairs={{0,24},{2,26},{4,28},{6,30},{8,0},{10,2},{12,4},{14,6},{16,8},{18,... | collective-permute-start | bytes 4718600 | tf_op jit(solution)/shard_map/ppermute | solution.py:212
  81.1 195.5 %collective-permute-start.4 = (bf16[512,3072]{1,0:T(8,128)(2,1)}, bf16[512,3072]{1,0:T(8,128)(2,1)}, u32[]{:S(2)}, u32[]{:S(2)}) collective-permute-start(bf16[512,3072]{1,0:T(8,128)(2,1)} %pad_maximum_fusion.6), channel_id=1, source_target_pairs={{0,16},{2,18},{4,20},{6,22},{8,24},{10,26},{12,28},{14,30},{16,0},... | collective-permute-start | bytes 9437192 | tf_op jit(solution)/shard_map/ppermute | solution.py:212
  82.2 24.7 %collective-permute-start = (bf16[512,1024]{1,0:T(8,128)(2,1)}, bf16[512,1024]{1,0:T(8,128)(2,1)}, u32[]{:S(2)}, u32[]{:S(2)}) collective-permute-start(bf16[512,1024]{1,0:T(8,128)(2,1)} %param.26), channel_id=1, source_target_pairs={{0,1},{1,0},{2,3},{3,2},{4,5},{5,4},{6,7},{7,6},{8,9},{9,8},{10,11... | collective-permute-start | bytes 3145736 | tf_op jit(solution)/shard_map/ppermute | solution.py:150
  86.6 649.6 %reduce-scatter.3.cloned.1.call-start = ((), (), s32[]{:S(2)}) async-start(), calls=%async_computation.3 | async-start | bytes 6684672 | tf_op jit(solution)/shard_map/reduce_scatter | solution.py:322
  90.6 230.8 %copy-start.15 = (f32[1024,64]{1,0:T(8,128)}, f32[1024,64]{1,0:T(8,128)S(1)}, u32[]{:S(2)}) copy-start(f32[1024,64]{1,0:T(8,128)S(1)} %get-tuple-element.133) | copy-start | bytes 786436
  108.9 181.0 %copy-start.64 = (f32[1024]{0:T(1024)}, f32[1024]{0:T(1024)S(1)}, u32[]{:S(2)}) copy-start(f32[1024]{0:T(1024)S(1)} %add_rsqrt_fusion.2) | copy-start | bytes 12292
  109.8 170.5 %copy-start.50 = (bf16[64,1024]{1,0:T(8,128)(2,1)S(1)}, bf16[64,1024]{1,0:T(8,128)(2,1)}, u32[]{:S(2)}) copy-start(bf16[64,1024]{1,0:T(8,128)(2,1)} %param.32) | copy-start | bytes 393220
  109.9 171.2 %copy-start.56 = (bf16[64,512]{1,0:T(8,128)(2,1)S(1)}, bf16[64,512]{1,0:T(8,128)(2,1)}, u32[]{:S(2)}) copy-start(bf16[64,512]{1,0:T(8,128)(2,1)} %param.33) | copy-start | bytes 196612
  109.9 171.8 %copy-start.57 = (bf16[64,512]{1,0:T(8,128)(2,1)S(1)}, bf16[64,512]{1,0:T(8,128)(2,1)}, u32[]{:S(2)}) copy-start(bf16[64,512]{1,0:T(8,128)(2,1)} %param.34) | copy-start | bytes 196612
  109.9 172.5 %copy-start.51 = (bf16[64,1024]{1,0:T(8,128)(2,1)S(1)}, bf16[64,1024]{1,0:T(8,128)(2,1)}, u32[]{:S(2)}) copy-start(bf16[64,1024]{1,0:T(8,128)(2,1)} %param.35) | copy-start | bytes 393220
  332.3 160.9 %copy-start.54 = (f32[1024,4]{0,1:T(4,128)}, f32[1024,4]{0,1:T(4,128)S(1)}, u32[]{:S(2)}) copy-start(f32[1024,4]{0,1:T(4,128)S(1)} %add_rsqrt_fusion.1) | copy-start | bytes 49156
  369.8 26.1 %collective-permute-start.5 = (bf16[512,1024]{1,0:T(8,128)(2,1)S(1)}, bf16[512,1024]{1,0:T(8,128)(2,1)S(1)}, u32[]{:S(2)}, u32[]{:S(2)}) collective-permute-start(bf16[512,1024]{1,0:T(8,128)(2,1)S(1)} %fusion.86), channel_id=1, source_target_pairs={{0,1},{1,0},{2,3},{3,2},{4,5},{5,4},{6,7},{7,6},{8,9},{9,8},{10,11... | collective-permute-start | bytes 3145736 | tf_op jit(solution)/shard_map/ppermute | solution.py:170
  371.4 47.0 %collective-permute-start.8 = (bf16[512,1024]{1,0:T(8,128)(2,1)S(1)}, bf16[512,1024]{1,0:T(8,128)(2,1)S(1)}, u32[]{:S(2)}, u32[]{:S(2)}) collective-permute-start(bf16[512,1024]{1,0:T(8,128)(2,1)S(1)} %copy-done.22), channel_id=1, source_target_pairs={{0,1},{1,0},{2,3},{3,2},{4,5},{5,4},{6,7},{7,6},{8,9},{9,8},{10,11... | collective-permute-start | bytes 3145736 | tf_op jit(solution)/shard_map/ppermute | solution.py:150
  399.4 90.6 %copy-start.10 = (f32[512,1024]{1,0:T(8,128)}, f32[512,1024]{1,0:T(8,128)S(1)}, u32[]{:S(2)}) copy-start(f32[512,1024]{1,0:T(8,128)S(1)} %get-tuple-element.139) | copy-start | bytes 6291460
  399.4 90.6 %copy-start.62 = (f32[512]{0:T(512)}, f32[512]{0:T(512)S(1)}, u32[]{:S(2)}) copy-start(f32[512]{0:T(512)S(1)} %add_rsqrt_fusion.3) | copy-start | bytes 6148
  400.9 39.2 %collective-permute-start.6 = (bf16[512,1024]{1,0:T(8,128)(2,1)}, bf16[512,1024]{1,0:T(8,128)(2,1)}, u32[]{:S(2)}, u32[]{:S(2)}) collective-permute-start(bf16[512,1024]{1,0:T(8,128)(2,1)} %multiply_convert_fusion.4), channel_id=1, source_target_pairs={{0,1},{1,0},{2,3},{3,2},{4,5},{5,4},{6,7},{7,6},{8,9},{9,8},{10,11... | collective-permute-start | bytes 3145736 | tf_op jit(solution)/shard_map/ppermute | solution.py:150
  462.9 24.3 %collective-permute-start.9 = (bf16[512,1024]{1,0:T(8,128)(2,1)S(1)}, bf16[512,1024]{1,0:T(8,128)(2,1)S(1)}, u32[]{:S(2)}, u32[]{:S(2)}) collective-permute-start(bf16[512,1024]{1,0:T(8,128)(2,1)S(1)} %add_convert_fusion.1), channel_id=1, source_target_pairs={{0,1},{1,0},{2,3},{3,2},{4,5},{5,4},{6,7},{7,6},{8,9},{9,8},{10,11... | collective-permute-start | bytes 3145736 | tf_op jit(solution)/shard_map/ppermute | solution.py:170
  491.7 23.6 %collective-permute-start.10 = (bf16[512,1024]{1,0:T(8,128)(2,1)}, bf16[512,1024]{1,0:T(8,128)(2,1)S(1)}, u32[]{:S(2)}, u32[]{:S(2)}) collective-permute-start(bf16[512,1024]{1,0:T(8,128)(2,1)} %fusion.133), channel_id=1, source_target_pairs={{0,1},{1,0},{2,3},{3,2},{4,5},{5,4},{6,7},{7,6},{8,9},{9,8},{10,11... | collective-permute-start | bytes 3145736 | tf_op jit(solution)/shard_map/ppermute | solution.py:150
  639.0 198.5 %reduce-scatter.5.cloned.1.call-start = ((), (), s32[]{:S(2)}) async-start(), calls=%async_computation.4 | async-start | bytes 10027008 | tf_op jit(solution)/shard_map/reduce_scatter | solution.py:285
  675.7 26.1 %collective-permute-start.11 = (bf16[512,1024]{1,0:T(8,128)(2,1)S(1)}, bf16[512,1024]{1,0:T(8,128)(2,1)S(1)}, u32[]{:S(2)}, u32[]{:S(2)}) collective-permute-start(bf16[512,1024]{1,0:T(8,128)(2,1)S(1)} %fusion.89), channel_id=1, source_target_pairs={{0,1},{1,0},{2,3},{3,2},{4,5},{5,4},{6,7},{7,6},{8,9},{9,8},{10,11... | collective-permute-start | bytes 3145736 | tf_op jit(solution)/shard_map/ppermute | solution.py:170
  681.3 42.7 %collective-permute-start.7 = (bf16[512,1024]{1,0:T(8,128)(2,1)S(1)}, bf16[512,1024]{1,0:T(8,128)(2,1)S(1)}, u32[]{:S(2)}, u32[]{:S(2)}) collective-permute-start(bf16[512,1024]{1,0:T(8,128)(2,1)S(1)} %fusion.83), channel_id=1, source_target_pairs={{0,1},{1,0},{2,3},{3,2},{4,5},{5,4},{6,7},{7,6},{8,9},{9,8},{10,11... | collective-permute-start | bytes 3145736 | tf_op jit(solution)/shard_map/ppermute | solution.py:170
  682.7 41.3 %copy-start.11 = (f32[512,1024]{1,0:T(8,128)S(1)}, f32[512,1024]{1,0:T(8,128)}, u32[]{:S(2)}) copy-start(f32[512,1024]{1,0:T(8,128)} %copy-done.10) | copy-start | bytes 6291460
  706.9 14.4 %collective-permute-start.12 = (f32[18,128]{1,0:T(8,128)S(1)}, f32[18,128]{1,0:T(8,128)S(1)}, u32[]{:S(2)}, u32[]{:S(2)}) collective-permute-start(f32[18,128]{1,0:T(8,128)S(1)} %maximum_bitcast_fusion.3), channel_id=1, source_target_pairs={{0,1},{1,0},{2,3},{3,2},{4,5},{5,4},{6,7},{7,6},{8,9},{9,8},{10,11... | collective-permute-start | bytes 27656 | tf_op jit(solution)/shard_map/ppermute | solution.py:139
  721.3 1.2 collective-permute-start.13
  722.6 4.2 collective-permute-start.14
  726.8 3.7 collective-permute-start.15
  730.5 4.6 collective-permute-start.16
  (88 other events, 713.2 us)
Sparse Core Ops, SparseCore 0:
  86.7 160.1 all-gather.1
  639.1 83.8 reduce-scatter.2
  727.1 110.3 reduce-scatter.4
